TPU v7x, 512 devices: a whole 4x4x16 slice. The times are simulated.
512 devices in a mesh: section: 32 (over z, core), seq: 16 (over x, y).
Axes of the slice: x: 4, y: 4, z: 16, core: 2. Of those that a mesh axis runs over, the one named last changes fastest.
Arguments:
- layer_input: bfloat16 [32, 3, 4096, 768], P('section', None, 'seq'), may hold values from -6 to 6
- grad_out: bfloat16 [32, 3, 4096, 768], P('section', None, 'seq'), may hold values from -6 to 6
- gate_weight: bfloat16 [768, 768], P('seq'), may hold values from -0.21875 to 0.21875
- mix_in_right: bfloat16 [64, 64, 64], P('seq'), may hold values from -0.75 to 0.75
- mix_in_left: bfloat16 [64, 64, 64], P('seq'), may hold values from -0.75 to 0.75
- mix_out_left: bfloat16 [64, 64, 64], P('seq'), may hold values from -0.75 to 0.75
- mix_out_right: bfloat16 [64, 64, 64], P('seq'), may hold values from -0.75 to 0.75
- kernel: bfloat16 [4096, 768], P('seq'), may hold values from -5 to 5
Outputs:
- input_grad: bfloat16 [32, 3, 4096, 768], P('section', None, 'seq')
- weight_grad: float32 [768, 768], P('seq')
- kernel_grad: bfloat16 [4096, 768], P('seq')
All inputs are finite; a program needn't handle non-finite values.
Results may differ from a plain program's by a relative error of at most 0.007.
Values may be sent and summed in bfloat16 or wider, within the bound.
A program may use at most 64 MiB of HBM per device.

v0:
```python
import math
import jax
import jax.numpy as jnp
from jax import lax
from jax.sharding import PartitionSpec as P

BATCH = 3
SEQ = 4096


def contract(form, left, right):
    return jnp.einsum(form, left, right, preferred_element_type=jnp.float32)


def forward_middle(spread, left_in, left_out, kern):
    second_mixed = contract("ija,baid->bijd", left_in, spread)
    weighted = (second_mixed * kern).astype(jnp.bfloat16)
    third_mixed = contract("ikj,bijd->bikd", left_out, weighted).astype(jnp.bfloat16)
    return (second_mixed, third_mixed)


def backward_middle(back_spread, second_mixed, left_in, left_out, kern):
    back_second = contract("ikj,bkid->bijd", left_out, back_spread)
    kernel_sum = jnp.sum(second_mixed * back_second, axis=0)
    back_weighted = (back_second * kern).astype(jnp.bfloat16)
    back_first = contract("ija,bijd->biad", left_in, back_weighted).astype(jnp.bfloat16)
    return (kernel_sum, back_first)


def local(
    layer_input,
    grad_out,
    gate_weight,
    mix_in_right,
    mix_in_left,
    mix_out_left,
    mix_out_right,
    kernel,
):
    count_batch = layer_input.shape[1]
    token_rows = layer_input.shape[2]
    width = layer_input.shape[3]
    groups = mix_in_right.shape[0]
    block_size = mix_in_right.shape[1]
    replicas = lax.axis_size("section")
    kern = kernel.reshape(groups, block_size, width).astype(jnp.float32)
    acts = layer_input[0].reshape(count_batch, groups, block_size, width)
    flat_input = layer_input[0].reshape(count_batch * token_rows, width)
    upstream = grad_out[0].reshape(count_batch * token_rows, width).astype(jnp.float32)
    weights = lax.all_gather(gate_weight, "seq", axis=0, tiled=True)
    preact = jnp.dot(flat_input, weights, preferred_element_type=jnp.float32)
    sigma = jax.nn.sigmoid(preact)
    swish = preact * sigma
    slope = sigma * (1.0 + preact * (1.0 - sigma))
    mix_grad = (
        (upstream * swish).astype(jnp.bfloat16).reshape(count_batch, groups, block_size, width)
    )
    first_mixed = contract("aic,bacd->baid", mix_in_right, acts).astype(jnp.bfloat16)
    back_third = contract("kmi,bkmd->bkid", mix_out_right, mix_grad).astype(jnp.bfloat16)
    spread = lax.all_to_all(first_mixed, "seq", split_axis=2, concat_axis=1, tiled=True)
    second_mixed, third_mixed = forward_middle(spread, mix_in_left, mix_out_left, kern)
    returned = lax.all_to_all(third_mixed, "seq", split_axis=2, concat_axis=1, tiled=True)
    back_spread = lax.all_to_all(back_third, "seq", split_axis=2, concat_axis=1, tiled=True)
    kernel_sum, back_first = backward_middle(
        back_spread, second_mixed, mix_in_left, mix_out_left, kern
    )
    back_return = lax.all_to_all(back_first, "seq", split_axis=2, concat_axis=1, tiled=True)
    mixed = contract("kmi,bikd->bkmd", mix_out_right, returned).reshape(
        count_batch * token_rows, width
    )
    gate_grad = (upstream * mixed * slope).astype(jnp.bfloat16)
    gate_part = lax.dot_general(
        gate_grad, weights, (((1,), (1,)), ((), ())), preferred_element_type=jnp.float32
    )
    weight_scale = 1.0 / math.sqrt(replicas * BATCH * SEQ)
    kernel_scale = 1.0 / math.sqrt(replicas * BATCH)
    term = lax.dot_general(
        flat_input, gate_grad, (((0,), (0,)), ((), ())), preferred_element_type=jnp.float32
    )
    weight_local = lax.psum_scatter(term * weight_scale, "seq", scatter_dimension=0, tiled=True)
    weight_grad, kernel_total = lax.psum((weight_local, kernel_sum * kernel_scale), "section")
    mix_part = contract("aic,biad->bacd", mix_in_right, back_return).reshape(
        count_batch * token_rows, width
    )
    input_grad = (
        (gate_part + mix_part).astype(jnp.bfloat16).reshape(1, count_batch, token_rows, width)
    )
    kernel_grad = kernel_total.astype(jnp.bfloat16).reshape(groups * block_size, width)
    return (input_grad, weight_grad, kernel_grad)


def solution(mesh):
    placed = (
        P("section", None, "seq", None),
        P("section", None, "seq", None),
        P("seq", None),
        P("seq", None, None),
        P("seq", None, None),
        P("seq", None, None),
        P("seq", None, None),
        P("seq", None),
    )
    return jax.shard_map(
        local,
        mesh=mesh,
        in_specs=placed,
        out_specs=(P("section", None, "seq", None), P("seq", None), P("seq", None)),
        check_vma=False,
    )
```

profile of v0, /device:TPU:2, one launch (start us, length us, event | category | flops | bytes accessed | tf_op | source)
XLA Modules:
  0.0 457.6 jit_solution(12352171297710613128)
XLA Ops:
  7.2 0.0 copy-start
  7.2 1.3 copy-done
  8.4 1.3 fusion.9
  9.7 1.9 copy.54
  11.7 0.0 copy-start.4
  11.7 9.5 %all-to-all-start = ((bf16[3,4,64,768]{3,1,0,2:T(4,128)(2,1)}), bf16[3,4,64,768]{3,1,0,2:T(4,128)(2,1)S(1)}, u32[]{:S(2)}, u32[]{:S(2)}) async-start(bf16[3,4,64,768]{3,1,0,2:T(4,128)(2,1)} %copy.54), calls=%async_computation | async-start | bytes 2359296 | tf_op jit(solution)/shard_map/all_to_all | solution.py:60
  21.2 0.0 all-gather.2.cloned.1.call-start
  21.2 0.7 all-gather.2.cloned.1.call-update
  21.9 0.0 reduce-scatter.4.cloned.1.call-start
  22.0 0.0 copy-done.4
  22.0 0.9 convert.3
  22.9 13.2 %all-to-all-done = bf16[3,4,64,768]{3,1,0,2:T(4,128)(2,1)S(1)} async-done(((bf16[3,4,64,768]{3,1,0,2:T(4,128)(2,1)}), bf16[3,4,64,768]{3,1,0,2:T(4,128)(2,1)S(1)}, u32[]{:S(2)}, u32[]{:S(2)}) %all-to-all-start) | async-done | bytes 1179680 | tf_op jit(solution)/shard_map/all_to_all | solution.py:60
  36.1 0.5 copy.99
  36.6 1.2 all_to_all.55
  37.8 0.0 copy-start.1
  37.8 0.0 copy-start.5
  37.8 1.8 fusion.23
  39.6 0.0 copy-done.1
  39.6 0.0 copy-done.5
  39.6 0.5 fusion.10
  40.1 0.9 copy.56
  41.1 22.2 %all_to_all.72 = bf16[3,4,64,768]{3,1,0,2:T(4,128)(2,1)S(1)} all-to-all(bf16[3,4,64,768]{3,1,0,2:T(4,128)(2,1)S(1)} %copy.56), channel_id=1, replica_groups=mesh['section'=32,'seq'=16] {'seq'}, dimensions={2} | all-to-all | bytes 2359296 | tf_op jit(solution)/shard_map/all_to_all | solution.py:62
  63.2 1.5 copy.98
  64.8 3.1 all_to_all.59
  67.9 1.8 convolution_bitcast_fusion
  69.7 1.6 copy.58
  71.2 18.5 %all-gather.2.cloned.1.call-done = bf16[768,768]{1,0:T(8,128)(2,1)} async-done(((bf16[48,768]{1,0:T(8,128)(2,1)}), bf16[768,768]{1,0:T(8,128)(2,1)}) %all-gather.2.cloned.1.call-update) | async-done | bytes 1179664 | tf_op jit(solution)/shard_map/all_gather | solution.py:50
  89.7 5.1 %fusion.1 = (bf16[768,768]{1,0:T(8,128)(2,1)S(1)}, bf16[768,768]{1,0:T(8,128)(2,1)}) fusion(f32[3,4,64,768]{3,2,1,0:T(8,128)} %copy.58, bf16[1,3,256,768]{3,2,1,0:T(8,128)(2,1)} %param.9, bf16[768,768]{1,0:T(8,128)(2,1)S(1)} %bitcast.123, bf16[768,768]{1,0:T(8,128)(2,1)} %all-gather.2.cloned.1.call-done), kind=kOutput, calls=%fused_computation.3 | convolution fusion | flops 914227200 | bytes 8257536 | tf_op jit(solution)/shard_map/dot_general | solution.py:51
  94.9 0.0 copy-start.7
  94.9 1.1 copy-done.7
  95.9 2.5 multiply_bitcast_fusion
  98.4 3.1 copy.86
  101.5 0.0 reduce-scatter.4.cloned.1.call-update
  101.5 1.8 fusion.7
  103.3 0.9 copy.61
  104.2 22.5 %all_to_all.73 = bf16[3,4,64,768]{3,1,0,2:T(4,128)(2,1)S(1)} all-to-all(bf16[3,4,64,768]{3,1,0,2:T(4,128)(2,1)S(1)} %copy.61), channel_id=1, replica_groups=mesh['section'=32,'seq'=16] {'seq'}, dimensions={2} | all-to-all | bytes 2359296 | tf_op jit(solution)/shard_map/all_to_all | solution.py:63
  126.8 1.5 copy.97
  128.3 3.2 all_to_all.63
  131.5 0.0 copy-start.2
  131.5 0.0 copy-start.6
  131.5 2.8 fusion.5
  134.3 0.0 copy-done.2
  134.3 0.0 copy-done.6
  134.3 0.5 fusion.8
  134.8 1.9 copy.65
  136.8 0.0 copy-start.3
  136.8 5.5 %all-to-all-start.3 = ((bf16[3,4,64,768]{3,1,0,2:T(4,128)(2,1)}), bf16[3,4,64,768]{3,1,0,2:T(4,128)(2,1)S(1)}, u32[]{:S(2)}, u32[]{:S(2)}) async-start(bf16[3,4,64,768]{3,1,0,2:T(4,128)(2,1)} %copy.65), calls=%async_computation.3 | async-start | bytes 2359296 | tf_op jit(solution)/shard_map/all_to_all | solution.py:67
  142.2 0.0 all-reduce.3.cloned.1.call-start
  142.3 0.0 copy-done.3
  142.3 1.0 broadcast_multiply_fusion
  143.2 100.1 %all-reduce.4 = bf16[4,64,768]{2,1,0:T(8,128)(2,1)} all-reduce(f32[4,64,768]{2,1,0:T(8,128)} %broadcast_multiply_fusion), channel_id=1, replica_groups=mesh['section'=32,'seq'=16] {'section'}, use_global_device_ids=true, to_apply=%region_3.0 | all-reduce | flops 196608 | bytes 1179648 | tf_op jit(solution)/shard_map/psum | solution.py:81
  243.3 0.0 all-to-all-done.3
  243.3 0.5 copy.96
  243.8 0.3 all_to_all.67
  244.2 1.4 convolution_bitcast_fusion.1
  245.5 0.2 copy.68
  245.7 0.0 reduce-scatter.4.cloned.1.call-done
  245.7 1.8 copy.87
  247.5 0.0 all-reduce.3.cloned.1.call-update
  247.6 3.8 fusion.3
  251.3 198.0 %all-reduce.3.cloned.1.call-done = f32[48,768]{0,1:T(8,128)} async-done(((f32[48,768]{0,1:T(8,128)}), f32[48,768]{0,1:T(8,128)}) %all-reduce.3.cloned.1.call-update) | async-done | bytes 147472 | tf_op jit(solution)/shard_map/psum | solution.py:81
  449.3 1.8 copy.69
Async XLA Ops:
  7.2 1.3 copy-start
  11.7 10.3 %copy-start.4 = (bf16[256,768]{1,0:T(8,128)(2,1)S(1)}, bf16[256,768]{1,0:T(8,128)(2,1)}, u32[]{:S(2)}) copy-start(bf16[256,768]{1,0:T(8,128)(2,1)} %param.15) | copy-start | bytes 1179652
  11.7 24.5 %all-to-all-start = ((bf16[3,4,64,768]{3,1,0,2:T(4,128)(2,1)}), bf16[3,4,64,768]{3,1,0,2:T(4,128)(2,1)S(1)}, u32[]{:S(2)}, u32[]{:S(2)}) async-start(bf16[3,4,64,768]{3,1,0,2:T(4,128)(2,1)} %copy.54), calls=%async_computation | async-start | bytes 2359296 | tf_op jit(solution)/shard_map/all_to_all | solution.py:60
  21.2 68.5 %all-gather.2.cloned.1.call-start = ((), (), s32[]{:S(2)}) async-start(), calls=%async_computation.5 | async-start | bytes 1253376 | tf_op jit(solution)/shard_map/all_gather | solution.py:50
  21.9 223.8 %reduce-scatter.4.cloned.1.call-start = ((), (), s32[]{:S(2)}) async-start(), calls=%async_computation.7 | async-start | bytes 2506752
  37.8 1.8 copy-start.1
  37.8 1.8 copy-start.5
  94.9 1.1 copy-start.7
  131.5 2.8 copy-start.2
  131.5 2.8 copy-start.6
  136.8 5.5 %copy-start.3 = (f32[4,64,768]{2,1,0:T(8,128)S(1)}, f32[4,64,768]{2,1,0:T(8,128)}, u32[]{:S(2)}) copy-start(f32[4,64,768]{2,1,0:T(8,128)} %get-tuple-element.17) | copy-start | bytes 2359300
  136.8 106.6 %all-to-all-start.3 = ((bf16[3,4,64,768]{3,1,0,2:T(4,128)(2,1)}), bf16[3,4,64,768]{3,1,0,2:T(4,128)(2,1)S(1)}, u32[]{:S(2)}, u32[]{:S(2)}) async-start(bf16[3,4,64,768]{3,1,0,2:T(4,128)(2,1)} %copy.65), calls=%async_computation.3 | async-start | bytes 2359296 | tf_op jit(solution)/shard_map/all_to_all | solution.py:67
  142.2 307.1 %all-reduce.3.cloned.1.call-start = ((), (), s32[]{:S(2)}) async-start(), calls=%async_computation.6 | async-start | bytes 786432 | tf_op jit(solution)/shard_map/psum | solution.py:81
Sparse Core Ops, SparseCore 0:
  25.1 64.5 all-gather.1
  101.6 98.0 reduce-scatter.3
  247.7 201.5 all-reduce.2
where the time goes:
time: 459 us; the launch traced here: 458 us
  waiting for transfers between devices  230 us (50%)
  blocking collectives  145 us (32%)
  local copies, waits for them, and re-layouts  28.3 us (6%)
  matrix products  23.3 us (5%)
  starting transfers between devices  15.1 us (3%)
  between operations  13.9 us (3%)
    psum x1, waiting for transfers between devices, local(): lax.psum((weight_local, kernel_sum * kernel_scale), 'section')  198 us
    psum x1, blocking collectives, local(): lax.psum((weight_local, kernel_sum * kernel_scale), 'section')  100 us
    all_to_all x1, blocking collectives, local(): lax.all_to_all(back_third, 'seq', split_axis=2, concat_axis=1, tiled=True)  22.5 us
    all_to_all x1, blocking collectives, local(): lax.all_to_all(third_mixed, 'seq', split_axis=2, concat_axis=1, tiled=True)  22.2 us
    all_gather x1, waiting for transfers between devices, local(): weights = lax.all_gather(gate_weight, 'seq', axis=0, tiled=True)  18.5 us
    all_to_all x1, waiting for transfers between devices, local(): lax.all_to_all(first_mixed, 'seq', split_axis=2, concat_axis=1, tiled=True)  13.2 us
    dot_general x8, matrix products, contract(): return jnp.einsum(form, left, right, preferred_element_type=jnp.float32)  11.8 us
    all_to_all x1, starting transfers between devices, local(): lax.all_to_all(first_mixed, 'seq', split_axis=2, concat_axis=1, tiled=True)  9.55 us
  transfers between devices with their start and end apart: 5, of which 3 were waited for; matrix products, arithmetic and copies ran while one was open for 6% of the time, Pallas kernels for 0%

commit v1 on v0

--- a/solution.py
+++ b/solution.py
@@ -47,7 +47,9 @@
     acts = layer_input[0].reshape(count_batch, groups, block_size, width)
     flat_input = layer_input[0].reshape(count_batch * token_rows, width)
     upstream = grad_out[0].reshape(count_batch * token_rows, width).astype(jnp.float32)
-    weights = lax.all_gather(gate_weight, "seq", axis=0, tiled=True)
+    weights = jnp.concatenate(
+        lax.all_to_all(jnp.stack([gate_weight] * lax.axis_size("seq")), "seq", 0, 0), axis=0
+    )
     preact = jnp.dot(flat_input, weights, preferred_element_type=jnp.float32)
     sigma = jax.nn.sigmoid(preact)
     swish = preact * sigma

time: 459 us -> 454 us (0.989)
  waiting for transfers between devices: 230 us -> 214 us
  starting transfers between devices: 15.1 us -> 20.6 us
    all_gather x1 -> x0, waiting for transfers between devices: 18.5 us -> none  [local(): weights = lax.all_gather(gate_weight, 'seq', axis=0, tiled=True)]
    all_to_all x0 -> x1, starting transfers between devices: none -> 5.69 us  [local(): lax.all_to_all(jnp.stack([gate_weight] * lax.axis_size('seq')), 'seq', 0, 0)]
    all_to_all x0 -> x1, waiting for transfers between devices: none -> 5.45 us  [local(): lax.all_to_all(jnp.stack([gate_weight] * lax.axis_size('seq')), 'seq', 0, 0)]
    psum x1, blocking collectives: 100 us -> 105 us  [local(): lax.psum((weight_local, kernel_sum * kernel_scale), 'section')]
  transfers between devices with their start and end apart: 5 -> 5, of which waited for: 3 -> 3; matrix products, arithmetic and copies ran while one was open for 6% -> 5% of each run, Pallas kernels for 0% -> 0%
where the time goes in v1:
time: 454 us; the launch traced here: 453 us
  waiting for transfers between devices  214 us (47%)
  blocking collectives  148 us (33%)
  local copies, waits for them, and re-layouts  30.7 us (7%)
  matrix products  23.2 us (5%)
  starting transfers between devices  20.6 us (5%)
  between operations  14.2 us (3%)
    psum x1, waiting for transfers between devices, local(): lax.psum((weight_local, kernel_sum * kernel_scale), 'section')  194 us
    psum x1, blocking collectives, local(): lax.psum((weight_local, kernel_sum * kernel_scale), 'section')  105 us
    all_to_all x1, blocking collectives, local(): lax.all_to_all(back_third, 'seq', split_axis=2, concat_axis=1, tiled=True)  21.6 us
    all_to_all x1, blocking collectives, local(): lax.all_to_all(third_mixed, 'seq', split_axis=2, concat_axis=1, tiled=True)  21.2 us
    all_to_all x1, waiting for transfers between devices, local(): lax.all_to_all(first_mixed, 'seq', split_axis=2, concat_axis=1, tiled=True)  14 us
    dot_general x8, matrix products, contract(): return jnp.einsum(form, left, right, preferred_element_type=jnp.float32)  11.8 us
    all_to_all x1, starting transfers between devices, local(): lax.all_to_all(first_mixed, 'seq', split_axis=2, concat_axis=1, tiled=True)  9.55 us
  transfers between devices with their start and end apart: 5, of which 3 were waited for; matrix products, arithmetic and copies ran while one was open for 5% of the time, Pallas kernels for 0%

profile of v1, /device:TPU:2, one launch (start us, length us, event | category | flops | bytes accessed | tf_op | source)
XLA Modules:
  0.0 452.6 jit_solution(11425798142141487661)
XLA Ops:
  7.2 0.0 copy-start
  7.2 1.3 copy-done
  8.4 1.3 fusion.9
  9.7 1.9 copy.54
  11.7 0.0 copy-start.4
  11.7 9.5 %all-to-all-start = ((bf16[3,4,64,768]{3,1,0,2:T(4,128)(2,1)}), bf16[3,4,64,768]{3,1,0,2:T(4,128)(2,1)S(1)}, u32[]{:S(2)}, u32[]{:S(2)}) async-start(bf16[3,4,64,768]{3,1,0,2:T(4,128)(2,1)} %copy.54), calls=%async_computation | async-start | bytes 2359296 | tf_op jit(solution)/shard_map/all_to_all | solution.py:62
  21.2 0.0 copy-done.4
  21.2 0.9 convert.3
  22.1 14.0 %all-to-all-done = bf16[3,4,64,768]{3,1,0,2:T(4,128)(2,1)S(1)} async-done(((bf16[3,4,64,768]{3,1,0,2:T(4,128)(2,1)}), bf16[3,4,64,768]{3,1,0,2:T(4,128)(2,1)S(1)}, u32[]{:S(2)}, u32[]{:S(2)}) %all-to-all-start) | async-done | bytes 1179680 | tf_op jit(solution)/shard_map/all_to_all | solution.py:62
  36.1 0.5 copy.99
  36.6 1.2 all_to_all.58
  37.8 0.0 copy-start.1
  37.8 0.0 copy-start.5
  37.8 1.8 fusion.23
  39.6 0.0 copy-done.1
  39.6 0.0 copy-done.5
  39.6 0.5 fusion.10
  40.1 0.9 copy.56
  41.1 0.0 copy-start.7
  41.1 21.2 %all_to_all.77 = bf16[3,4,64,768]{3,1,0,2:T(4,128)(2,1)} all-to-all(bf16[3,4,64,768]{3,1,0,2:T(4,128)(2,1)S(1)} %copy.56), channel_id=1, replica_groups=mesh['section'=32,'seq'=16] {'seq'}, dimensions={2} | all-to-all | bytes 2359296 | tf_op jit(solution)/shard_map/all_to_all | solution.py:64
  62.3 0.0 copy-done.7
  62.3 1.1 stack.2
  63.4 5.7 %all-to-all-start.2 = ((bf16[16,48,768]{2,1,0:T(8,128)(2,1)}), bf16[16,48,768]{2,1,0:T(8,128)(2,1)}, u32[]{:S(2)}, u32[]{:S(2)}) async-start(bf16[16,48,768]{2,1,0:T(8,128)(2,1)} %stack.2), calls=%async_computation.2 | async-start | bytes 2359296 | tf_op jit(solution)/shard_map/all_to_all | solution.py:51
  69.1 0.0 reduce-scatter.4.cloned.1.call-start
  69.1 2.8 copy.98
  71.9 3.1 all_to_all.62
  75.1 1.8 convolution_bitcast_fusion
  76.8 1.6 copy.58
  78.4 5.5 %all-to-all-done.2 = bf16[16,48,768]{2,1,0:T(8,128)(2,1)} async-done(((bf16[16,48,768]{2,1,0:T(8,128)(2,1)}), bf16[16,48,768]{2,1,0:T(8,128)(2,1)}, u32[]{:S(2)}, u32[]{:S(2)}) %all-to-all-start.2) | async-done | bytes 1179680 | tf_op jit(solution)/shard_map/all_to_all | solution.py:51
  83.8 5.1 %fusion.1 = (bf16[768,768]{1,0:T(8,128)(2,1)S(1)}, bf16[768,768]{1,0:T(8,128)(2,1)}) fusion(f32[3,4,64,768]{3,2,1,0:T(8,128)} %copy.58, bf16[1,3,256,768]{3,2,1,0:T(8,128)(2,1)} %param.9, bf16[768,768]{1,0:T(8,128)(2,1)S(1)} %bitcast.124, bf16[768,768]{1,0:T(8,128)(2,1)} %bitcast.21), kind=kOutput, calls=%fused_computation.3 | convolution fusion | flops 914227200 | bytes 8257536 | tf_op jit(solution)/shard_map/dot_general | solution.py:53
  89.0 0.0 copy-start.8
  89.0 1.1 copy-done.8
  90.1 2.5 multiply_bitcast_fusion
  92.6 3.1 copy.86
  95.6 0.0 reduce-scatter.4.cloned.1.call-update
  95.7 1.8 fusion.7
  97.5 0.9 copy.61
  98.4 21.6 %all_to_all.78 = bf16[3,4,64,768]{3,1,0,2:T(4,128)(2,1)S(1)} all-to-all(bf16[3,4,64,768]{3,1,0,2:T(4,128)(2,1)S(1)} %copy.61), channel_id=1, replica_groups=mesh['section'=32,'seq'=16] {'seq'}, dimensions={2} | all-to-all | bytes 2359296 | tf_op jit(solution)/shard_map/all_to_all | solution.py:65
  120.0 1.5 copy.97
  121.6 3.2 all_to_all.67
  124.7 0.0 copy-start.2
  124.7 0.0 copy-start.6
  124.7 2.8 fusion.5
  127.5 0.0 copy-done.2
  127.5 0.0 copy-done.6
  127.5 0.5 fusion.8
  128.1 1.9 copy.65
  130.0 0.0 copy-start.3
  130.0 5.3 %all-to-all-start.4 = ((bf16[3,4,64,768]{3,1,0,2:T(4,128)(2,1)}), bf16[3,4,64,768]{3,1,0,2:T(4,128)(2,1)S(1)}, u32[]{:S(2)}, u32[]{:S(2)}) async-start(bf16[3,4,64,768]{3,1,0,2:T(4,128)(2,1)} %copy.65), calls=%async_computation.4 | async-start | bytes 2359296 | tf_op jit(solution)/shard_map/all_to_all | solution.py:69
  135.3 0.0 all-reduce.3.cloned.1.call-start
  135.3 0.0 copy-done.3
  135.3 1.0 broadcast_multiply_fusion
  136.3 105.4 %all-reduce.4 = bf16[4,64,768]{2,1,0:T(8,128)(2,1)} all-reduce(f32[4,64,768]{2,1,0:T(8,128)} %broadcast_multiply_fusion), channel_id=1, replica_groups=mesh['section'=32,'seq'=16] {'section'}, use_global_device_ids=true, to_apply=%region_3.0 | all-reduce | flops 196608 | bytes 1179648 | tf_op jit(solution)/shard_map/psum | solution.py:83
  241.7 0.0 all-to-all-done.4
  241.7 0.5 copy.96
  242.2 0.3 all_to_all.71
  242.6 1.4 convolution_bitcast_fusion.1
  243.9 0.2 copy.68
  244.1 0.0 reduce-scatter.4.cloned.1.call-done
  244.1 1.8 copy.87
  245.9 0.0 all-reduce.3.cloned.1.call-update
  246.0 3.8 fusion.3
  249.7 194.3 %all-reduce.3.cloned.1.call-done = f32[48,768]{0,1:T(8,128)} async-done(((f32[48,768]{0,1:T(8,128)}), f32[48,768]{0,1:T(8,128)}) %all-reduce.3.cloned.1.call-update) | async-done | bytes 147472 | tf_op jit(solution)/shard_map/psum | solution.py:83
  444.0 1.8 copy.69
Async XLA Ops:
  7.2 1.3 copy-start
  11.7 9.6 %copy-start.4 = (bf16[256,768]{1,0:T(8,128)(2,1)S(1)}, bf16[256,768]{1,0:T(8,128)(2,1)}, u32[]{:S(2)}) copy-start(bf16[256,768]{1,0:T(8,128)(2,1)} %param.15) | copy-start | bytes 1179652
  11.7 24.5 %all-to-all-start = ((bf16[3,4,64,768]{3,1,0,2:T(4,128)(2,1)}), bf16[3,4,64,768]{3,1,0,2:T(4,128)(2,1)S(1)}, u32[]{:S(2)}, u32[]{:S(2)}) async-start(bf16[3,4,64,768]{3,1,0,2:T(4,128)(2,1)} %copy.54), calls=%async_computation | async-start | bytes 2359296 | tf_op jit(solution)/shard_map/all_to_all | solution.py:62
  37.8 1.8 copy-start.1
  37.8 1.8 copy-start.5
  41.1 21.2 %copy-start.7 = (bf16[48,768]{1,0:T(8,128)(2,1)S(1)}, bf16[48,768]{1,0:T(8,128)(2,1)}, u32[]{:S(2)}) copy-start(bf16[48,768]{1,0:T(8,128)(2,1)} %param.10) | copy-start | bytes 221188
  63.4 20.4 %all-to-all-start.2 = ((bf16[16,48,768]{2,1,0:T(8,128)(2,1)}), bf16[16,48,768]{2,1,0:T(8,128)(2,1)}, u32[]{:S(2)}, u32[]{:S(2)}) async-start(bf16[16,48,768]{2,1,0:T(8,128)(2,1)} %stack.2), calls=%async_computation.2 | async-start | bytes 2359296 | tf_op jit(solution)/shard_map/all_to_all | solution.py:51
  69.1 175.0 %reduce-scatter.4.cloned.1.call-start = ((), (), s32[]{:S(2)}) async-start(), calls=%async_computation.7 | async-start | bytes 2506752
  89.0 1.1 copy-start.8
  124.7 2.8 copy-start.2
  124.7 2.8 copy-start.6
  130.0 5.3 %copy-start.3 = (f32[4,64,768]{2,1,0:T(8,128)S(1)}, f32[4,64,768]{2,1,0:T(8,128)}, u32[]{:S(2)}) copy-start(f32[4,64,768]{2,1,0:T(8,128)} %get-tuple-element.17) | copy-start | bytes 2359300
  130.0 111.7 %all-to-all-start.4 = ((bf16[3,4,64,768]{3,1,0,2:T(4,128)(2,1)}), bf16[3,4,64,768]{3,1,0,2:T(4,128)(2,1)S(1)}, u32[]{:S(2)}, u32[]{:S(2)}) async-start(bf16[3,4,64,768]{3,1,0,2:T(4,128)(2,1)} %copy.65), calls=%async_computation.4 | async-start | bytes 2359296 | tf_op jit(solution)/shard_map/all_to_all | solution.py:69
  135.3 308.7 %all-reduce.3.cloned.1.call-start = ((), (), s32[]{:S(2)}) async-start(), calls=%async_computation.6 | async-start | bytes 786432 | tf_op jit(solution)/shard_map/psum | solution.py:83
Sparse Core Ops, SparseCore 0:
  95.8 99.1 reduce-scatter.3
  246.1 197.8 all-reduce.2
